TPU v7x, 256 devices: a whole 4x4x8 slice. The times are simulated.
256 devices in a mesh: tm: 32 (over z, y_hi, core), space: 8 (over y_lo, x).
Axes of the slice: x: 4, y: 4 (y_hi: 2, y_lo: 2; y = y_hi * 2 + y_lo), z: 8, core: 2. Of those that a mesh axis runs over, the one named last changes fastest.
Arguments:
- model: float32 [32, 8192, 1024], P('tm', 'space'), may hold values from -6 to 6
- kernels: float32 [3, 600, 8192], P(None, None, ('space', 'tm')), may hold values from -0.0390625 to 0.0390625
Outputs:
- data: float32 [32, 600, 1024], P('tm', None, 'space')
All inputs are finite; a program needn't handle non-finite values.
Results may differ from a plain program's by a relative error of at most 0.0003.
Values sent between devices are 32-bit elements; how exact they have to be, the bound alone decides.
A program may use at most 64 MiB of HBM per device.

v0:
```python
import jax
import jax.numpy as jnp
from jax import lax
from jax.sharding import PartitionSpec as P


def passed_along(block, axis, distance):
    devices = range(lax.axis_size(axis))
    route = [(i - distance, i) for i in devices if i - distance in devices]
    return lax.ppermute(block, axis, route)


def on_device(model, kernels):
    local_model = model[0]
    lag_count = kernels.shape[0]
    products = jnp.einsum(
        "lsp,pc->lsc",
        lax.all_gather(kernels, "tm", axis=2, tiled=True),
        local_model,
        precision=lax.Precision.HIGHEST,
        preferred_element_type=jnp.float32,
    )
    running = products[lag_count - 1]
    for lag_index in range(lag_count - 2, -1, -1):
        running = passed_along(running, "tm", 1) + products[lag_index]
    result = lax.psum_scatter(running, "space", scatter_dimension=1, tiled=True)
    return result[None]


def solution(mesh):
    return jax.shard_map(
        on_device,
        mesh=mesh,
        in_specs=(P("tm", "space", None), P(None, None, ("space", "tm"))),
        out_specs=P("tm", None, "space"),
        check_vma=False,
    )
```

profile of v0, /device:TPU:32, one launch (start us, length us, event | category | flops | bytes accessed | tf_op | source)
XLA Modules:
  0.0 261.7 jit_solution(11356863142729187960)
XLA Ops:
  6.5 0.0 all-gather.2.cloned.1.call-start
  6.5 0.7 all-gather.2.cloned.1.call-update
  7.3 0.0 reduce-scatter.2.cloned.1.call-start
  7.3 104.9 %all-gather.2.cloned.1.call-done = f32[3,600,1024]{1,2,0:T(8,128)} async-done(((f32[3,600,32]{1,2,0:T(8,128)}), f32[3,600,1024]{1,2,0:T(8,128)}) %all-gather.2.cloned.1.call-update) | async-done | bytes 7372816 | tf_op jit(solution)/shard_map/all_gather | solution.py:18
  112.2 27.5 %fusion = f32[3,600,1024]{2,1,0:T(8,128)S(1)} fusion(f32[3,600,1024]{1,2,0:T(8,128)} %all-gather.2.cloned.1.call-done, f32[1,1024,1024]{2,1,0:T(8,128)} %param.2), kind=kOutput, calls=%fused_computation | convolution fusion | flops 22649241600 | bytes 18939904 | tf_op jit(solution)/shard_map/lsp,pc->lsc/dot_general | solution.py:16
  139.7 0.2 slice_bitcast_fusion.2
  139.9 2.2 collective-permute-start
  142.1 31.5 %collective-permute-done = f32[600,1024]{1,0:T(8,128)S(1)} collective-permute-done((f32[600,1024]{1,0:T(8,128)S(1)}, f32[600,1024]{1,0:T(8,128)S(1)}, u32[]{:S(2)}, u32[]{:S(2)}) %collective-permute-start) | collective-permute-done | bytes 2457632 | tf_op jit(solution)/shard_map/ppermute | solution.py:10
  173.5 0.5 fusion.3
  174.0 1.9 collective-permute-start.1
  175.9 31.7 %collective-permute-done.1 = f32[600,1024]{1,0:T(8,128)S(1)} collective-permute-done((f32[600,1024]{1,0:T(8,128)S(1)}, f32[600,1024]{1,0:T(8,128)S(1)}, u32[]{:S(2)}, u32[]{:S(2)}) %collective-permute-start.1) | collective-permute-done | bytes 2457632 | tf_op jit(solution)/shard_map/ppermute | solution.py:10
  207.6 1.9 fusion.2
  209.5 0.0 reduce-scatter.2.cloned.1.call-update
  209.6 45.3 %reduce-scatter.2.cloned.1.call-done = f32[600,128]{1,0:T(8,128)} async-done(((f32[600,1024]{1,0:T(8,128)}), f32[600,128]{1,0:T(8,128)}) %reduce-scatter.2.cloned.1.call-update) | async-done | bytes 307216 | tf_op jit(solution)/shard_map/reduce_scatter | solution.py:26
Async XLA Ops:
  6.5 105.7 %all-gather.2.cloned.1.call-start = ((), (), s32[]{:S(2)}) async-start(), calls=%async_computation.1 | async-start | bytes 8110080 | tf_op jit(solution)/shard_map/all_gather | solution.py:18
  7.3 247.6 %reduce-scatter.2.cloned.1.call-start = ((), (), s32[]{:S(2)}) async-start(), calls=%async_computation.2 | async-start | bytes 2764800 | tf_op jit(solution)/shard_map/reduce_scatter | solution.py:26
  139.9 33.6 %collective-permute-start = (f32[600,1024]{1,0:T(8,128)S(1)}, f32[600,1024]{1,0:T(8,128)S(1)}, u32[]{:S(2)}, u32[]{:S(2)}) collective-permute-start(f32[600,1024]{1,0:T(8,128)S(1)} %slice_bitcast_fusion.2), channel_id=1, source_target_pairs={{0,8},{8,16},{16,24},{24,32},{32,40},{40,48},{48,56},{56,64},{64,7... | collective-permute-start | bytes 7372808 | tf_op jit(solution)/shard_map/ppermute | solution.py:10
  174.0 33.6 %collective-permute-start.1 = (f32[600,1024]{1,0:T(8,128)S(1)}, f32[600,1024]{1,0:T(8,128)S(1)}, u32[]{:S(2)}, u32[]{:S(2)}) collective-permute-start(f32[600,1024]{1,0:T(8,128)S(1)} %fusion.3), channel_id=1, source_target_pairs={{0,8},{8,16},{16,24},{24,32},{32,40},{40,48},{48,56},{56,64},{64,7... | collective-permute-start | bytes 7372808 | tf_op jit(solution)/shard_map/ppermute | solution.py:10
Sparse Core Ops, SparseCore 0:
  10.1 102.0 all-gather.1
  209.7 45.1 reduce-scatter.1
where the time goes:
time: 262 us
  waiting for transfers between devices  214 us (82%)
  matrix products  27.5 us (10%)
  between operations  13.4 us (5%)
  starting transfers between devices  4.12 us (2%)
    all_gather x1, waiting for transfers between devices, on_device(): lax.all_gather(kernels, 'tm', axis=2, tiled=True)  105 us
    ppermute x2, waiting for transfers between devices, passed_along(): return lax.ppermute(block, axis, route)  63.1 us
    reduce_scatter x1, waiting for transfers between devices, on_device(): result = lax.psum_scatter(running, 'space', scatter_dimension=1, tiled=True)  45.3 us
    dot_general x1, matrix products, on_device(): jnp.einsum('lsp,pc->lsc', lax.all_gather(kernels, 'tm', axis=2, tiled=Tru...  27.5 us
  transfers between devices with their start and end apart: 4, of which 4 were waited for; matrix products, arithmetic and copies ran while one was open for 0% of the time, Pallas kernels for 0%

commit v1 on v0

--- a/solution.py
+++ b/solution.py
@@ -2,6 +2,11 @@
 import jax.numpy as jnp
 from jax import lax
 from jax.sharding import PartitionSpec as P
+
+
+def gather_over(block, axis, d):
+    sent = jnp.stack([block] * lax.axis_size(axis))
+    return jnp.concatenate(lax.all_to_all(sent, axis, 0, 0), axis=d)
 
 
 def passed_along(block, axis, distance):
@@ -15,7 +20,7 @@
     lag_count = kernels.shape[0]
     products = jnp.einsum(
         "lsp,pc->lsc",
-        lax.all_gather(kernels, "tm", axis=2, tiled=True),
+        gather_over(kernels, "tm", 2),
         local_model,
         precision=lax.Precision.HIGHEST,
         preferred_element_type=jnp.float32,

time: 262 us -> 348 us (1.33)
  blocking collectives: 0 us -> 186 us
  waiting for transfers between devices: 214 us -> 108 us
  local copies, waits for them, and re-layouts: 0.17 us -> 4.25 us
    all_to_all x0 -> x1, blocking collectives: none -> 186 us  [gather_over(): return jnp.concatenate(lax.all_to_all(sent, axis, 0, 0), axis=d)]
    all_gather x1 -> x0, waiting for transfers between devices: 105 us -> none  [on_device(): lax.all_gather(kernels, 'tm', axis=2, tiled=True)]
  transfers between devices with their start and end apart: 4 -> 3, of which waited for: 4 -> 3; matrix products, arithmetic and copies ran while one was open for 0% -> 0% of each run, Pallas kernels for 0% -> 0%
where the time goes in v1:
time: 348 us; the launch traced here: 347 us
  blocking collectives  186 us (53%)
  waiting for transfers between devices  108 us (31%)
  matrix products  29.4 us (8%)
  between operations  13.4 us (4%)
  local copies, waits for them, and re-layouts  4.25 us (1%)
  starting transfers between devices  3.84 us (1%)
    all_to_all x1, blocking collectives, gather_over(): return jnp.concatenate(lax.all_to_all(sent, axis, 0, 0), axis=d)  186 us
    ppermute x2, waiting for transfers between devices, passed_along(): return lax.ppermute(block, axis, route)  63.4 us
    reduce_scatter x1, waiting for transfers between devices, on_device(): result = lax.psum_scatter(running, 'space', scatter_dimension=1, tiled=True)  44.7 us
    dot_general x1, matrix products, on_device(): jnp.einsum('lsp,pc->lsc', gather_over(kernels, 'tm', 2), local_model, pre...  29.4 us
  transfers between devices with their start and end apart: 3, of which 3 were waited for; matrix products, arithmetic and copies ran while one was open for 0% of the time, Pallas kernels for 0%

profile of v1, /device:TPU:32, one launch (start us, length us, event | category | flops | bytes accessed | tf_op | source)
XLA Modules:
  0.0 347.4 jit_solution(11646270161508642864)
XLA Ops:
  6.5 0.0 reduce-scatter.2.cloned.1.call-start
  6.5 1.9 stack.2
  8.4 186.0 %all_to_all.5 = f32[32,3,600,32]{2,3,1,0:T(8,128)S(1)} all-to-all(f32[32,3,600,32]{2,3,1,0:T(8,128)S(1)} %stack.2), channel_id=1, replica_groups=mesh['tm'=32,'space'=8] {'tm'}, dimensions={0} | all-to-all | bytes 14745600 | tf_op jit(solution)/shard_map/all_to_all | solution.py:9
  194.4 0.0 copy-start
  194.4 0.7 copy.5
  195.1 1.5 copy-done
  196.6 29.4 %fusion = f32[3,600,1024]{2,1,0:T(8,128)S(1)} fusion(f32[3,600,1024]{1,2,0:T(8,128)S(1)} %bitcast.19, f32[1,1024,1024]{2,1,0:T(8,128)S(1)} %copy-done), kind=kOutput, calls=%fused_computation | convolution fusion | flops 22649241600 | bytes 18939904 | tf_op jit(solution)/shard_map/lsp,pc->lsc/dot_general | solution.py:21
  226.0 0.2 slice_bitcast_fusion.2
  226.2 1.9 collective-permute-start
  228.1 31.7 %collective-permute-done = f32[600,1024]{1,0:T(8,128)S(1)} collective-permute-done((f32[600,1024]{1,0:T(8,128)S(1)}, f32[600,1024]{1,0:T(8,128)S(1)}, u32[]{:S(2)}, u32[]{:S(2)}) %collective-permute-start) | collective-permute-done | bytes 2457632 | tf_op jit(solution)/shard_map/ppermute | solution.py:15
  259.8 0.5 fusion.3
  260.3 1.9 collective-permute-start.1
  262.2 31.7 %collective-permute-done.1 = f32[600,1024]{1,0:T(8,128)S(1)} collective-permute-done((f32[600,1024]{1,0:T(8,128)S(1)}, f32[600,1024]{1,0:T(8,128)S(1)}, u32[]{:S(2)}, u32[]{:S(2)}) %collective-permute-start.1) | collective-permute-done | bytes 2457632 | tf_op jit(solution)/shard_map/ppermute | solution.py:15
  293.9 1.9 fusion.2
  295.8 0.0 reduce-scatter.2.cloned.1.call-update
  295.8 44.7 %reduce-scatter.2.cloned.1.call-done = f32[600,128]{1,0:T(8,128)} async-done(((f32[600,1024]{1,0:T(8,128)}), f32[600,128]{1,0:T(8,128)}) %reduce-scatter.2.cloned.1.call-update) | async-done | bytes 307216 | tf_op jit(solution)/shard_map/reduce_scatter | solution.py:31
Async XLA Ops:
  6.5 334.0 %reduce-scatter.2.cloned.1.call-start = ((), (), s32[]{:S(2)}) async-start(), calls=%async_computation.2 | async-start | bytes 2764800 | tf_op jit(solution)/shard_map/reduce_scatter | solution.py:31
  194.4 2.2 copy-start
  226.2 33.6 %collective-permute-start = (f32[600,1024]{1,0:T(8,128)S(1)}, f32[600,1024]{1,0:T(8,128)S(1)}, u32[]{:S(2)}, u32[]{:S(2)}) collective-permute-start(f32[600,1024]{1,0:T(8,128)S(1)} %slice_bitcast_fusion.2), channel_id=1, source_target_pairs={{0,8},{8,16},{16,24},{24,32},{32,40},{40,48},{48,56},{56,64},{64,7... | collective-permute-start | bytes 7372808 | tf_op jit(solution)/shard_map/ppermute | solution.py:15
  260.3 33.6 %collective-permute-start.1 = (f32[600,1024]{1,0:T(8,128)S(1)}, f32[600,1024]{1,0:T(8,128)S(1)}, u32[]{:S(2)}, u32[]{:S(2)}) collective-permute-start(f32[600,1024]{1,0:T(8,128)S(1)} %fusion.3), channel_id=1, source_target_pairs={{0,8},{8,16},{16,24},{24,32},{32,40},{40,48},{48,56},{56,64},{64,7... | collective-permute-start | bytes 7372808 | tf_op jit(solution)/shard_map/ppermute | solution.py:15
Sparse Core Ops, SparseCore 0:
  296.0 44.5 reduce-scatter.1
